TPU v7x, 32 devices: a whole 2x2x4 slice. The times are simulated.
32 devices in a mesh: grp: 2 (over y), ja: 4 (over z), ia: 4 (over x, core).
Axes of the slice: x: 2, y: 2, z: 4, core: 2. Of those that a mesh axis runs over, the one named last changes fastest.
Arguments:
- pos_vel: float32 [6, 8192], P(None, ('grp', 'ja')), parts along dimension 1, may hold values from -6 to 6
- acc_jerk: float32 [6, 8192], P(None, ('grp', 'ja')), parts along dimension 1, may hold values from -6 to 6
- mass: float32 [8192], P(('grp', 'ja')), parts along dimension 0, may hold values from 7.324219e-05 to 0.0007324219
- age: float32 [8192], P(('grp', 'ja')), parts along dimension 0, may hold values from 0.125 to 0.5
- active_local: int32 [12288], P(('grp', 'ia')), parts along dimension 0, may hold values from 0 to 1023
- active_owner: int32 [12288], P(('grp', 'ia')), parts along dimension 0, may hold values from 0 to 3
Outputs:
- state: float32 [6, 12288], P(None, ('grp', 'ia')), parts along dimension 1
- forces: float32 [7, 12288], P(None, ('grp', 'ia')), parts along dimension 1
There are 2 independent parts, one for each index of `grp`. A program takes and returns all parts, laid end to end along the dimension named above; each array names one. Nothing has to cross between parts.
All inputs are finite; a program needn't handle non-finite values.
Results may differ from a plain program's by a relative error of at most 0.0003.
Values sent between devices are 32-bit elements; how exact they have to be, the bound alone decides.
No kernel may reach another device: no remote copies, remote signals or barrier semaphores. Data moves between devices by JAX's collectives and lax.ppermute only.
A program may use at most 64 MiB of HBM per device.

v0:
```python
import jax
import jax.numpy as jnp
from jax import lax
from jax.sharding import PartitionSpec as P

soften = 0.0004


def predict(pos_vel, acc_jerk, age):
    position = pos_vel[0:3]
    velocity = pos_vel[3:6]
    accel = acc_jerk[0:3]
    jolt = acc_jerk[3:6]
    step_len = age[None, :]
    new_pos = position + step_len * (velocity + step_len * (accel * 0.5 + step_len * jolt / 6.0))
    new_vel = velocity + step_len * (accel + step_len * jolt * 0.5)
    return jnp.concatenate([new_pos, new_vel], axis=0)


def pair_terms(targets, sources, masses):
    delta_pos = sources[0:3, :, None] - targets[0:3, None, :]
    delta_vel = sources[3:6, :, None] - targets[3:6, None, :]
    dist_sq = jnp.sum(delta_pos * delta_pos, axis=0) + soften
    inverse = lax.rsqrt(dist_sq)
    inv_sq = inverse * inverse
    weighted = masses[:, None] * inverse
    weighted_cube = weighted * inv_sq
    radial = 3.0 * jnp.sum(delta_pos * delta_vel, axis=0) * inv_sq
    accel = jnp.sum(weighted_cube[None] * delta_pos, axis=1)
    jolt = jnp.sum(weighted_cube[None] * (delta_vel - radial[None] * delta_pos), axis=1)
    potential = -jnp.sum(weighted, axis=0)
    return jnp.concatenate([accel, jolt, potential[None]], axis=0)


def block_terms(targets, sources, masses):
    count = targets.shape[1]
    width = min(512, count)
    nblocks = count // width
    src_count = sources.shape[1]
    src_width = min(512, src_count)
    src_blocks = src_count // src_width
    source_pieces = sources.reshape(6, src_blocks, src_width).transpose(1, 0, 2)
    mass_pieces = masses.reshape(src_blocks, src_width)
    pieces = targets.reshape(6, nblocks, width).transpose(1, 0, 2)

    def one_block(piece):

        def accumulate(total, parts):
            return (total + pair_terms(piece, parts[0], parts[1]), None)

        total, unused = lax.scan(
            accumulate, jnp.zeros((7, width), jnp.float32), (source_pieces, mass_pieces)
        )
        return total

    results = lax.map(one_block, pieces)
    return results.transpose(1, 0, 2).reshape(7, count)


def correct(history, forces):
    pred_pos = history[0:3]
    pred_vel = history[3:6]
    old_acc = history[6:9]
    old_jolt = history[9:12]
    step_len = history[12:13]
    new_acc = forces[0:3]
    new_jolt = forces[3:6]
    differ = old_acc - new_acc
    square = step_len * step_len
    cubed = square * step_len
    fourth = square * square
    fifth = fourth * step_len
    second = (-6.0 * differ - step_len * (4.0 * old_jolt + 2.0 * new_jolt)) / square
    third = (12.0 * differ + 6.0 * step_len * (old_jolt + new_jolt)) / cubed
    position = pred_pos + fourth / 24.0 * second + fifth / 120.0 * third
    velocity = pred_vel + cubed / 6.0 * second + fourth / 24.0 * third
    return jnp.concatenate([position, velocity], axis=0)


def local(pos_vel, acc_jerk, mass, age, active_local, active_owner):
    shard_rank = lax.axis_index("ja")
    predicted = predict(pos_vel, acc_jerk, age)
    stacked = jnp.concatenate([predicted, acc_jerk, age[None, :]], axis=0)
    picked = jnp.take(stacked, active_local, axis=1)
    owned = active_owner == shard_rank
    contrib = jnp.where(owned[None, :], picked, 0.0)
    history = lax.psum(contrib, "ja")
    partial_value = block_terms(history[0:6], predicted, mass)
    forces = lax.psum(partial_value, "ja")
    state = correct(history, forces)
    return (state, forces)


def solution(mesh):
    return jax.shard_map(
        local,
        mesh=mesh,
        in_specs=(
            P(None, ("grp", "ja")),
            P(None, ("grp", "ja")),
            P(("grp", "ja")),
            P(("grp", "ja")),
            P(("grp", "ia")),
            P(("grp", "ia")),
        ),
        out_specs=(P(None, ("grp", "ia")), P(None, ("grp", "ia"))),
        check_vma=False,
    )
```

profile of v0, /device:TPU:0, one launch (start us, length us, event | category | flops | bytes accessed | tf_op | source)
XLA Modules:
  0.0 92.8 jit_solution(16712219660879244907)
XLA Ops:
  7.2 0.0 all-reduce.2.cloned.1.call-start
  7.2 0.7 compare_select_fusion
  7.9 0.9 multiply_add_fusion.1
  8.8 0.8 pad_maximum_fusion
  9.6 0.0 copy-start.2
  9.6 0.0 copy-start.3
  9.6 0.2 copy.93
  9.8 0.0 copy-start.4
  9.9 2.6 %gather_fusion = f32[1536,13]{1,0:T(8,128)S(1)} fusion(f32[13,1024]{0,1:T(8,128)S(1)} %copy.93, s32[2048]{0:T(1024)S(1)} %pad_clamp_fusion), kind=kCustom, calls=%fused_computation | custom fusion | bytes 165888 | tf_op jit(solution)/shard_map/jit(_take)/gather | solution.py:84
  12.5 0.3 copy.94
  12.7 0.0 copy-done.2
  12.7 0.0 copy-done.3
  12.8 0.7 select_bitcast_fusion
  13.4 0.0 all-reduce.2.cloned.1.call-update
  13.4 0.0 copy-done.4
  13.5 37.3 %all-reduce.2.cloned.1.call-done = f32[13,1536]{1,0:T(8,128)} async-done(((f32[13,1536]{1,0:T(8,128)}), f32[13,1536]{1,0:T(8,128)}) %all-reduce.2.cloned.1.call-update) | async-done | bytes 79888 | tf_op jit(solution)/shard_map/psum | solution.py:87
  50.8 0.8 slice.71
  51.6 0.0 copy-start
  51.6 15.3 %while.22 = (s32[]{:T(128)}, f32[3,7,512]{2,1,0:T(8,128)S(1)}, f32[3,6,512]{2,1,0:T(8,128)S(1)}, f32[2,512]{1,0:T(2,128)S(1)}, f32[2,6,512]{2,1,0:T(8,128)S(1)},...) while((s32[]{:T(128)}, f32[3,7,512]{2,1,0:T(8,128)S(1)}, f32[3,6,512]{2,1,0:T(8,128)S(1)}, ...), condition=%wide.region_9.10_spmd, body=%wide.region_1.9_spmd.sunk | while | flops 12332038 | bytes 8612156 | solution.py:56
  51.6 5.1 %while.23 = (s32[]{:T(128)}, f32[7,512]{1,0:T(8,128)S(1)}, f32[2,512]{1,0:T(2,128)S(1)}, f32[2,6,512]{2,1,0:T(8,128)S(1)}, f32[6,512]{1,0:T(8,128)S(1)}, /*index=5*/s32[]{:T(128)}, s32[]{:T(128)}, s32[]{}) while((s32[]{:T(128)}, f32[7,512]{1,0:T(8,128)S(1)}, f32[2,512]{1,0:T(2,128)S(1)}, f32[2,6,512]{2,1,0:T(8,128)S(1)}, ...), condition=%wide.region_8.8_spmd.clone, body=%wide.region_2.7_spmd.clone.sunk | while | flops 12332036 | bytes 8554623 | solution.py:51
  51.7 1.0 %fusion.13 = (f32[512,512]{1,0:T(8,128)S(1)}, f32[512,512]{1,0:T(8,128)S(1)}) fusion(f32[3,512]{1,0:T(4,128)S(1)} %get-tuple-element.214, f32[3,512]{1,0:T(4,128)S(1)} %get-tuple-element.215, f32[3,512]{1,0:T(4,128)S(1)} %get-tuple-element.216, f32[3,512]{1,0:T(4,128)S(1)} %get-tuple-element.217), kind=kLoop, calls=%fused_computation.10.clone.1 | loop fusion | flops 4194304 | bytes 2121728 | tf_op jit(solution)/shard_map/while/body/eval_jaxpr/while/body/eval_jaxpr/reduce_sum | solution.py:28
  52.6 0.3 multiply_multiply_fusion.5
  53.0 1.1 %fusion.14 = (f32[3,512]{1,0:T(4,128)S(1)}, f32[3,512]{1,0:T(4,128)S(1)}) fusion(f32[512,512]{1,0:T(8,128)S(1)} %get-tuple-element.221, f32[3,512]{1,0:T(4,128)S(1)} %get-tuple-element.216, f32[3,512]{1,0:T(4,128)S(1)} %get-tuple-element.217, f32[512,512]{1,0:T(8,128)S(1)} %get-tuple-element.222, f32[3,512]{1,0:T(4,128)S(1)} %get-tuple-element.214, ...), kind=kLoop, calls=%fused_computation.9.clone.1 | loop fusion | flops 6288384 | bytes 2134016 | tf_op jit(solution)/shard_map/while/body/eval_jaxpr/while/body/eval_jaxpr/reduce_sum | solution.py:29
  54.2 1.0 %fusion.13 = (f32[512,512]{1,0:T(8,128)S(1)}, f32[512,512]{1,0:T(8,128)S(1)}) fusion(f32[3,512]{1,0:T(4,128)S(1)} %get-tuple-element.214, f32[3,512]{1,0:T(4,128)S(1)} %get-tuple-element.215, f32[3,512]{1,0:T(4,128)S(1)} %get-tuple-element.216, f32[3,512]{1,0:T(4,128)S(1)} %get-tuple-element.217), kind=kLoop, calls=%fused_computation.10.clone.1 | loop fusion | flops 4194304 | bytes 2121728 | tf_op jit(solution)/shard_map/while/body/eval_jaxpr/while/body/eval_jaxpr/reduce_sum | solution.py:28
  55.2 0.3 multiply_multiply_fusion.5
  55.5 1.1 %fusion.14 = (f32[3,512]{1,0:T(4,128)S(1)}, f32[3,512]{1,0:T(4,128)S(1)}) fusion(f32[512,512]{1,0:T(8,128)S(1)} %get-tuple-element.221, f32[3,512]{1,0:T(4,128)S(1)} %get-tuple-element.216, f32[3,512]{1,0:T(4,128)S(1)} %get-tuple-element.217, f32[512,512]{1,0:T(8,128)S(1)} %get-tuple-element.222, f32[3,512]{1,0:T(4,128)S(1)} %get-tuple-element.214, ...), kind=kLoop, calls=%fused_computation.9.clone.1 | loop fusion | flops 6288384 | bytes 2134016 | tf_op jit(solution)/shard_map/while/body/eval_jaxpr/while/body/eval_jaxpr/reduce_sum | solution.py:29
  56.7 5.1 %while.23 = (s32[]{:T(128)}, f32[7,512]{1,0:T(8,128)S(1)}, f32[2,512]{1,0:T(2,128)S(1)}, f32[2,6,512]{2,1,0:T(8,128)S(1)}, f32[6,512]{1,0:T(8,128)S(1)}, /*index=5*/s32[]{:T(128)}, s32[]{:T(128)}, s32[]{}) while((s32[]{:T(128)}, f32[7,512]{1,0:T(8,128)S(1)}, f32[2,512]{1,0:T(2,128)S(1)}, f32[2,6,512]{2,1,0:T(8,128)S(1)}, ...), condition=%wide.region_8.8_spmd.clone, body=%wide.region_2.7_spmd.clone.sunk | while | flops 12332036 | bytes 8554623 | solution.py:51
  56.8 1.0 %fusion.13 = (f32[512,512]{1,0:T(8,128)S(1)}, f32[512,512]{1,0:T(8,128)S(1)}) fusion(f32[3,512]{1,0:T(4,128)S(1)} %get-tuple-element.214, f32[3,512]{1,0:T(4,128)S(1)} %get-tuple-element.215, f32[3,512]{1,0:T(4,128)S(1)} %get-tuple-element.216, f32[3,512]{1,0:T(4,128)S(1)} %get-tuple-element.217), kind=kLoop, calls=%fused_computation.10.clone.1 | loop fusion | flops 4194304 | bytes 2121728 | tf_op jit(solution)/shard_map/while/body/eval_jaxpr/while/body/eval_jaxpr/reduce_sum | solution.py:28
  57.8 0.3 multiply_multiply_fusion.5
  58.1 1.1 %fusion.14 = (f32[3,512]{1,0:T(4,128)S(1)}, f32[3,512]{1,0:T(4,128)S(1)}) fusion(f32[512,512]{1,0:T(8,128)S(1)} %get-tuple-element.221, f32[3,512]{1,0:T(4,128)S(1)} %get-tuple-element.216, f32[3,512]{1,0:T(4,128)S(1)} %get-tuple-element.217, f32[512,512]{1,0:T(8,128)S(1)} %get-tuple-element.222, f32[3,512]{1,0:T(4,128)S(1)} %get-tuple-element.214, ...), kind=kLoop, calls=%fused_computation.9.clone.1 | loop fusion | flops 6288384 | bytes 2134016 | tf_op jit(solution)/shard_map/while/body/eval_jaxpr/while/body/eval_jaxpr/reduce_sum | solution.py:29
  59.3 1.0 %fusion.13 = (f32[512,512]{1,0:T(8,128)S(1)}, f32[512,512]{1,0:T(8,128)S(1)}) fusion(f32[3,512]{1,0:T(4,128)S(1)} %get-tuple-element.214, f32[3,512]{1,0:T(4,128)S(1)} %get-tuple-element.215, f32[3,512]{1,0:T(4,128)S(1)} %get-tuple-element.216, f32[3,512]{1,0:T(4,128)S(1)} %get-tuple-element.217), kind=kLoop, calls=%fused_computation.10.clone.1 | loop fusion | flops 4194304 | bytes 2121728 | tf_op jit(solution)/shard_map/while/body/eval_jaxpr/while/body/eval_jaxpr/reduce_sum | solution.py:28
  60.3 0.3 multiply_multiply_fusion.5
  60.6 1.1 %fusion.14 = (f32[3,512]{1,0:T(4,128)S(1)}, f32[3,512]{1,0:T(4,128)S(1)}) fusion(f32[512,512]{1,0:T(8,128)S(1)} %get-tuple-element.221, f32[3,512]{1,0:T(4,128)S(1)} %get-tuple-element.216, f32[3,512]{1,0:T(4,128)S(1)} %get-tuple-element.217, f32[512,512]{1,0:T(8,128)S(1)} %get-tuple-element.222, f32[3,512]{1,0:T(4,128)S(1)} %get-tuple-element.214, ...), kind=kLoop, calls=%fused_computation.9.clone.1 | loop fusion | flops 6288384 | bytes 2134016 | tf_op jit(solution)/shard_map/while/body/eval_jaxpr/while/body/eval_jaxpr/reduce_sum | solution.py:29
  61.8 5.1 %while.23 = (s32[]{:T(128)}, f32[7,512]{1,0:T(8,128)S(1)}, f32[2,512]{1,0:T(2,128)S(1)}, f32[2,6,512]{2,1,0:T(8,128)S(1)}, f32[6,512]{1,0:T(8,128)S(1)}, /*index=5*/s32[]{:T(128)}, s32[]{:T(128)}, s32[]{}) while((s32[]{:T(128)}, f32[7,512]{1,0:T(8,128)S(1)}, f32[2,512]{1,0:T(2,128)S(1)}, f32[2,6,512]{2,1,0:T(8,128)S(1)}, ...), condition=%wide.region_8.8_spmd.clone, body=%wide.region_2.7_spmd.clone.sunk | while | flops 12332036 | bytes 8554623 | solution.py:51
  61.9 1.0 %fusion.13 = (f32[512,512]{1,0:T(8,128)S(1)}, f32[512,512]{1,0:T(8,128)S(1)}) fusion(f32[3,512]{1,0:T(4,128)S(1)} %get-tuple-element.214, f32[3,512]{1,0:T(4,128)S(1)} %get-tuple-element.215, f32[3,512]{1,0:T(4,128)S(1)} %get-tuple-element.216, f32[3,512]{1,0:T(4,128)S(1)} %get-tuple-element.217), kind=kLoop, calls=%fused_computation.10.clone.1 | loop fusion | flops 4194304 | bytes 2121728 | tf_op jit(solution)/shard_map/while/body/eval_jaxpr/while/body/eval_jaxpr/reduce_sum | solution.py:28
  62.9 0.3 multiply_multiply_fusion.5
  63.2 1.1 %fusion.14 = (f32[3,512]{1,0:T(4,128)S(1)}, f32[3,512]{1,0:T(4,128)S(1)}) fusion(f32[512,512]{1,0:T(8,128)S(1)} %get-tuple-element.221, f32[3,512]{1,0:T(4,128)S(1)} %get-tuple-element.216, f32[3,512]{1,0:T(4,128)S(1)} %get-tuple-element.217, f32[512,512]{1,0:T(8,128)S(1)} %get-tuple-element.222, f32[3,512]{1,0:T(4,128)S(1)} %get-tuple-element.214, ...), kind=kLoop, calls=%fused_computation.9.clone.1 | loop fusion | flops 6288384 | bytes 2134016 | tf_op jit(solution)/shard_map/while/body/eval_jaxpr/while/body/eval_jaxpr/reduce_sum | solution.py:29
  64.4 1.0 %fusion.13 = (f32[512,512]{1,0:T(8,128)S(1)}, f32[512,512]{1,0:T(8,128)S(1)}) fusion(f32[3,512]{1,0:T(4,128)S(1)} %get-tuple-element.214, f32[3,512]{1,0:T(4,128)S(1)} %get-tuple-element.215, f32[3,512]{1,0:T(4,128)S(1)} %get-tuple-element.216, f32[3,512]{1,0:T(4,128)S(1)} %get-tuple-element.217), kind=kLoop, calls=%fused_computation.10.clone.1 | loop fusion | flops 4194304 | bytes 2121728 | tf_op jit(solution)/shard_map/while/body/eval_jaxpr/while/body/eval_jaxpr/reduce_sum | solution.py:28
  65.4 0.3 multiply_multiply_fusion.5
  65.7 1.1 %fusion.14 = (f32[3,512]{1,0:T(4,128)S(1)}, f32[3,512]{1,0:T(4,128)S(1)}) fusion(f32[512,512]{1,0:T(8,128)S(1)} %get-tuple-element.221, f32[3,512]{1,0:T(4,128)S(1)} %get-tuple-element.216, f32[3,512]{1,0:T(4,128)S(1)} %get-tuple-element.217, f32[512,512]{1,0:T(8,128)S(1)} %get-tuple-element.222, f32[3,512]{1,0:T(4,128)S(1)} %get-tuple-element.214, ...), kind=kLoop, calls=%fused_computation.9.clone.1 | loop fusion | flops 6288384 | bytes 2134016 | tf_op jit(solution)/shard_map/while/body/eval_jaxpr/while/body/eval_jaxpr/reduce_sum | solution.py:29
  66.9 18.2 %psum.15 = f32[7,1536]{1,0:T(8,128)S(1)} all-reduce(f32[7,1536]{1,0:T(8,128)S(1)} %bitcast.36), channel_id=1, replica_groups=mesh['grp'=2,'ja'=4,'ia'=4] {'ja'}, use_global_device_ids=true, to_apply=%region_10.11 | all-reduce | flops 10752 | bytes 86016 | tf_op jit(solution)/shard_map/psum | solution.py:89
  85.1 0.0 copy-done
  85.1 0.0 copy-start.1
  85.1 0.1 multiply_reduce_fusion.3
  85.2 0.1 fusion.6
  85.3 0.6 pad_maximum_fusion.1
  86.0 0.0 copy-done.1
  (45 shorter events, 0.4 us)
Async XLA Ops:
  7.2 43.6 %all-reduce.2.cloned.1.call-start = ((), (), s32[]{:S(2)}) async-start(), calls=%async_computation | async-start | bytes 196608 | tf_op jit(solution)/shard_map/psum | solution.py:87
  9.6 3.1 %copy-start.2 = (s32[1536]{0:T(1024)S(1)}, s32[1536]{0:T(1024)}, u32[]{:S(2)}) copy-start(s32[1536]{0:T(1024)} %param.14) | copy-start | bytes 18436
  9.6 3.1 %copy-start.3 = (s32[1536]{0:T(1024)S(1)}, s32[1536]{0:T(1024)}, u32[]{:S(2)}) copy-start(s32[1536]{0:T(1024)} %param.15) | copy-start | bytes 18436
  9.8 3.6 %copy-start.4 = (f32[1024]{0:T(1024)S(1)}, f32[1024]{0:T(1024)}, u32[]{:S(2)}) copy-start(f32[1024]{0:T(1024)} %param.12) | copy-start | bytes 12292
  51.6 33.5 %copy-start = (f32[13,1536]{1,0:T(8,128)S(1)}, f32[13,1536]{1,0:T(8,128)}, u32[]{:S(2)}) copy-start(f32[13,1536]{1,0:T(8,128)} %all-reduce.2.cloned.1.call-done) | copy-start | bytes 239620
  85.1 0.9 copy-start.1
Sparse Core Ops, SparseCore 0:
  13.5 37.1 all-reduce.1
where the time goes:
time: 93.2 us; the launch traced here: 92.8 us
  waiting for transfers between devices  37.3 us (40%)
  other arithmetic  18.5 us (20%)
  blocking collectives  18.2 us (20%)
  between operations  14.2 us (15%)
  local copies, waits for them, and re-layouts  4.12 us (4%)
    psum x1, waiting for transfers between devices, local(): history = lax.psum(contrib, 'ja')  37.3 us
    psum x1, blocking collectives, local(): forces = lax.psum(partial_value, 'ja')  18.2 us
    reduce_sum x6, other arithmetic, pair_terms(): accel = jnp.sum(weighted_cube[None] * delta_pos, axis=1)  6.74 us
    reduce_sum x6, other arithmetic, pair_terms(): radial = 3.0 * jnp.sum(delta_pos * delta_vel, axis=0) * inv_sq  5.85 us
    gather x2, local copies, waits for them, and re-layouts, local(): picked = jnp.take(stacked, active_local, axis=1)  2.86 us
  transfers between devices with their start and end apart: 1, of which 1 were waited for; matrix products, arithmetic and copies ran while one was open for 0% of the time, Pallas kernels for 0%

commit v1 on v0

--- a/solution.py
+++ b/solution.py
@@ -86,7 +86,8 @@
     contrib = jnp.where(owned[None, :], picked, 0.0)
     history = lax.psum(contrib, "ja")
     partial_value = block_terms(history[0:6], predicted, mass)
-    forces = lax.psum(partial_value, "ja")
+    shards = lax.all_gather(partial_value, "ja", axis=0, tiled=False)
+    forces = shards.sum(axis=0)
     state = correct(history, forces)
     return (state, forces)
 

time: 93.2 us -> 89 us (0.955)
  blocking collectives: 18.2 us -> 14 us
    psum x1 -> x0, blocking collectives: 18.2 us -> none  [local(): forces = lax.psum(partial_value, 'ja')]
    all_gather x0 -> x1, blocking collectives: none -> 14 us  [local(): shards = lax.all_gather(partial_value, 'ja', axis=0, tiled=False)]
where the time goes in v1:
time: 89 us; the launch traced here: 88.6 us
  waiting for transfers between devices  37.3 us (42%)
  other arithmetic  18.5 us (21%)
  between operations  14.2 us (16%)
  blocking collectives  14 us (16%)
  local copies, waits for them, and re-layouts  4.12 us (5%)
    psum x1, waiting for transfers between devices, local(): history = lax.psum(contrib, 'ja')  37.3 us
    all_gather x1, blocking collectives, local(): shards = lax.all_gather(partial_value, 'ja', axis=0, tiled=False)  14 us
    reduce_sum x6, other arithmetic, pair_terms(): accel = jnp.sum(weighted_cube[None] * delta_pos, axis=1)  6.74 us
    reduce_sum x6, other arithmetic, pair_terms(): radial = 3.0 * jnp.sum(delta_pos * delta_vel, axis=0) * inv_sq  5.85 us
    gather x2, local copies, waits for them, and re-layouts, local(): picked = jnp.take(stacked, active_local, axis=1)  2.86 us
    mul x6, other arithmetic, pair_terms(): weighted_cube = weighted * inv_sq  1.86 us
  transfers between devices with their start and end apart: 1, of which 1 were waited for; matrix products, arithmetic and copies ran while one was open for 0% of the time, Pallas kernels for 0%

profile of v1, /device:TPU:0, one launch (start us, length us, event | category | flops | bytes accessed | tf_op | source)
XLA Modules:
  0.0 88.6 jit_solution(1240960630054169977)
XLA Ops:
  7.2 0.0 all-reduce.2.cloned.1.call-start
  7.2 0.7 compare_select_fusion
  7.9 0.9 multiply_add_fusion.1
  8.8 0.8 pad_maximum_fusion
  9.6 0.0 copy-start.2
  9.6 0.0 copy-start.3
  9.6 0.2 copy.109
  9.8 0.0 copy-start.4
  9.9 2.6 %gather_fusion = f32[1536,13]{1,0:T(8,128)S(1)} fusion(f32[13,1024]{0,1:T(8,128)S(1)} %copy.109, s32[2048]{0:T(1024)S(1)} %pad_clamp_fusion), kind=kCustom, calls=%fused_computation | custom fusion | bytes 165888 | tf_op jit(solution)/shard_map/jit(_take)/gather | solution.py:84
  12.5 0.3 copy.110
  12.7 0.0 copy-done.2
  12.7 0.0 copy-done.3
  12.8 0.7 select_bitcast_fusion
  13.4 0.0 all-reduce.2.cloned.1.call-update
  13.4 0.0 copy-done.4
  13.5 37.3 %all-reduce.2.cloned.1.call-done = f32[13,1536]{1,0:T(8,128)} async-done(((f32[13,1536]{1,0:T(8,128)}), f32[13,1536]{1,0:T(8,128)}) %all-reduce.2.cloned.1.call-update) | async-done | bytes 79888 | tf_op jit(solution)/shard_map/psum | solution.py:87
  50.8 0.8 slice.71
  51.6 0.0 copy-start
  51.6 15.3 %while.22 = (s32[]{:T(128)}, f32[3,7,512]{2,1,0:T(8,128)S(1)}, f32[3,6,512]{2,1,0:T(8,128)S(1)}, f32[2,512]{1,0:T(2,128)S(1)}, f32[2,6,512]{2,1,0:T(8,128)S(1)},...) while((s32[]{:T(128)}, f32[3,7,512]{2,1,0:T(8,128)S(1)}, f32[3,6,512]{2,1,0:T(8,128)S(1)}, ...), condition=%wide.region_9.10_spmd, body=%wide.region_1.9_spmd.sunk | while | flops 12332038 | bytes 8612156 | solution.py:56
  51.6 5.1 %while.23 = (s32[]{:T(128)}, f32[7,512]{1,0:T(8,128)S(1)}, f32[2,512]{1,0:T(2,128)S(1)}, f32[2,6,512]{2,1,0:T(8,128)S(1)}, f32[6,512]{1,0:T(8,128)S(1)}, /*index=5*/s32[]{:T(128)}, s32[]{:T(128)}, s32[]{}) while((s32[]{:T(128)}, f32[7,512]{1,0:T(8,128)S(1)}, f32[2,512]{1,0:T(2,128)S(1)}, f32[2,6,512]{2,1,0:T(8,128)S(1)}, ...), condition=%wide.region_8.8_spmd.clone, body=%wide.region_2.7_spmd.clone.sunk | while | flops 12332036 | bytes 8554623 | solution.py:51
  51.7 1.0 %fusion.13 = (f32[512,512]{1,0:T(8,128)S(1)}, f32[512,512]{1,0:T(8,128)S(1)}) fusion(f32[3,512]{1,0:T(4,128)S(1)} %get-tuple-element.212, f32[3,512]{1,0:T(4,128)S(1)} %get-tuple-element.213, f32[3,512]{1,0:T(4,128)S(1)} %get-tuple-element.214, f32[3,512]{1,0:T(4,128)S(1)} %get-tuple-element.215), kind=kLoop, calls=%fused_computation.10.clone.1 | loop fusion | flops 4194304 | bytes 2121728 | tf_op jit(solution)/shard_map/while/body/eval_jaxpr/while/body/eval_jaxpr/reduce_sum | solution.py:28
  52.6 0.3 multiply_multiply_fusion.5
  53.0 1.1 %fusion.14 = (f32[3,512]{1,0:T(4,128)S(1)}, f32[3,512]{1,0:T(4,128)S(1)}) fusion(f32[512,512]{1,0:T(8,128)S(1)} %get-tuple-element.219, f32[3,512]{1,0:T(4,128)S(1)} %get-tuple-element.214, f32[3,512]{1,0:T(4,128)S(1)} %get-tuple-element.215, f32[512,512]{1,0:T(8,128)S(1)} %get-tuple-element.220, f32[3,512]{1,0:T(4,128)S(1)} %get-tuple-element.212, ...), kind=kLoop, calls=%fused_computation.9.clone.1 | loop fusion | flops 6288384 | bytes 2134016 | tf_op jit(solution)/shard_map/while/body/eval_jaxpr/while/body/eval_jaxpr/reduce_sum | solution.py:29
  54.2 1.0 %fusion.13 = (f32[512,512]{1,0:T(8,128)S(1)}, f32[512,512]{1,0:T(8,128)S(1)}) fusion(f32[3,512]{1,0:T(4,128)S(1)} %get-tuple-element.212, f32[3,512]{1,0:T(4,128)S(1)} %get-tuple-element.213, f32[3,512]{1,0:T(4,128)S(1)} %get-tuple-element.214, f32[3,512]{1,0:T(4,128)S(1)} %get-tuple-element.215), kind=kLoop, calls=%fused_computation.10.clone.1 | loop fusion | flops 4194304 | bytes 2121728 | tf_op jit(solution)/shard_map/while/body/eval_jaxpr/while/body/eval_jaxpr/reduce_sum | solution.py:28
  55.2 0.3 multiply_multiply_fusion.5
  55.5 1.1 %fusion.14 = (f32[3,512]{1,0:T(4,128)S(1)}, f32[3,512]{1,0:T(4,128)S(1)}) fusion(f32[512,512]{1,0:T(8,128)S(1)} %get-tuple-element.219, f32[3,512]{1,0:T(4,128)S(1)} %get-tuple-element.214, f32[3,512]{1,0:T(4,128)S(1)} %get-tuple-element.215, f32[512,512]{1,0:T(8,128)S(1)} %get-tuple-element.220, f32[3,512]{1,0:T(4,128)S(1)} %get-tuple-element.212, ...), kind=kLoop, calls=%fused_computation.9.clone.1 | loop fusion | flops 6288384 | bytes 2134016 | tf_op jit(solution)/shard_map/while/body/eval_jaxpr/while/body/eval_jaxpr/reduce_sum | solution.py:29
  56.7 5.1 %while.23 = (s32[]{:T(128)}, f32[7,512]{1,0:T(8,128)S(1)}, f32[2,512]{1,0:T(2,128)S(1)}, f32[2,6,512]{2,1,0:T(8,128)S(1)}, f32[6,512]{1,0:T(8,128)S(1)}, /*index=5*/s32[]{:T(128)}, s32[]{:T(128)}, s32[]{}) while((s32[]{:T(128)}, f32[7,512]{1,0:T(8,128)S(1)}, f32[2,512]{1,0:T(2,128)S(1)}, f32[2,6,512]{2,1,0:T(8,128)S(1)}, ...), condition=%wide.region_8.8_spmd.clone, body=%wide.region_2.7_spmd.clone.sunk | while | flops 12332036 | bytes 8554623 | solution.py:51
  56.8 1.0 %fusion.13 = (f32[512,512]{1,0:T(8,128)S(1)}, f32[512,512]{1,0:T(8,128)S(1)}) fusion(f32[3,512]{1,0:T(4,128)S(1)} %get-tuple-element.212, f32[3,512]{1,0:T(4,128)S(1)} %get-tuple-element.213, f32[3,512]{1,0:T(4,128)S(1)} %get-tuple-element.214, f32[3,512]{1,0:T(4,128)S(1)} %get-tuple-element.215), kind=kLoop, calls=%fused_computation.10.clone.1 | loop fusion | flops 4194304 | bytes 2121728 | tf_op jit(solution)/shard_map/while/body/eval_jaxpr/while/body/eval_jaxpr/reduce_sum | solution.py:28
  57.8 0.3 multiply_multiply_fusion.5
  58.1 1.1 %fusion.14 = (f32[3,512]{1,0:T(4,128)S(1)}, f32[3,512]{1,0:T(4,128)S(1)}) fusion(f32[512,512]{1,0:T(8,128)S(1)} %get-tuple-element.219, f32[3,512]{1,0:T(4,128)S(1)} %get-tuple-element.214, f32[3,512]{1,0:T(4,128)S(1)} %get-tuple-element.215, f32[512,512]{1,0:T(8,128)S(1)} %get-tuple-element.220, f32[3,512]{1,0:T(4,128)S(1)} %get-tuple-element.212, ...), kind=kLoop, calls=%fused_computation.9.clone.1 | loop fusion | flops 6288384 | bytes 2134016 | tf_op jit(solution)/shard_map/while/body/eval_jaxpr/while/body/eval_jaxpr/reduce_sum | solution.py:29
  59.3 1.0 %fusion.13 = (f32[512,512]{1,0:T(8,128)S(1)}, f32[512,512]{1,0:T(8,128)S(1)}) fusion(f32[3,512]{1,0:T(4,128)S(1)} %get-tuple-element.212, f32[3,512]{1,0:T(4,128)S(1)} %get-tuple-element.213, f32[3,512]{1,0:T(4,128)S(1)} %get-tuple-element.214, f32[3,512]{1,0:T(4,128)S(1)} %get-tuple-element.215), kind=kLoop, calls=%fused_computation.10.clone.1 | loop fusion | flops 4194304 | bytes 2121728 | tf_op jit(solution)/shard_map/while/body/eval_jaxpr/while/body/eval_jaxpr/reduce_sum | solution.py:28
  60.3 0.3 multiply_multiply_fusion.5
  60.6 1.1 %fusion.14 = (f32[3,512]{1,0:T(4,128)S(1)}, f32[3,512]{1,0:T(4,128)S(1)}) fusion(f32[512,512]{1,0:T(8,128)S(1)} %get-tuple-element.219, f32[3,512]{1,0:T(4,128)S(1)} %get-tuple-element.214, f32[3,512]{1,0:T(4,128)S(1)} %get-tuple-element.215, f32[512,512]{1,0:T(8,128)S(1)} %get-tuple-element.220, f32[3,512]{1,0:T(4,128)S(1)} %get-tuple-element.212, ...), kind=kLoop, calls=%fused_computation.9.clone.1 | loop fusion | flops 6288384 | bytes 2134016 | tf_op jit(solution)/shard_map/while/body/eval_jaxpr/while/body/eval_jaxpr/reduce_sum | solution.py:29
  61.8 5.1 %while.23 = (s32[]{:T(128)}, f32[7,512]{1,0:T(8,128)S(1)}, f32[2,512]{1,0:T(2,128)S(1)}, f32[2,6,512]{2,1,0:T(8,128)S(1)}, f32[6,512]{1,0:T(8,128)S(1)}, /*index=5*/s32[]{:T(128)}, s32[]{:T(128)}, s32[]{}) while((s32[]{:T(128)}, f32[7,512]{1,0:T(8,128)S(1)}, f32[2,512]{1,0:T(2,128)S(1)}, f32[2,6,512]{2,1,0:T(8,128)S(1)}, ...), condition=%wide.region_8.8_spmd.clone, body=%wide.region_2.7_spmd.clone.sunk | while | flops 12332036 | bytes 8554623 | solution.py:51
  61.9 1.0 %fusion.13 = (f32[512,512]{1,0:T(8,128)S(1)}, f32[512,512]{1,0:T(8,128)S(1)}) fusion(f32[3,512]{1,0:T(4,128)S(1)} %get-tuple-element.212, f32[3,512]{1,0:T(4,128)S(1)} %get-tuple-element.213, f32[3,512]{1,0:T(4,128)S(1)} %get-tuple-element.214, f32[3,512]{1,0:T(4,128)S(1)} %get-tuple-element.215), kind=kLoop, calls=%fused_computation.10.clone.1 | loop fusion | flops 4194304 | bytes 2121728 | tf_op jit(solution)/shard_map/while/body/eval_jaxpr/while/body/eval_jaxpr/reduce_sum | solution.py:28
  62.9 0.3 multiply_multiply_fusion.5
  63.2 1.1 %fusion.14 = (f32[3,512]{1,0:T(4,128)S(1)}, f32[3,512]{1,0:T(4,128)S(1)}) fusion(f32[512,512]{1,0:T(8,128)S(1)} %get-tuple-element.219, f32[3,512]{1,0:T(4,128)S(1)} %get-tuple-element.214, f32[3,512]{1,0:T(4,128)S(1)} %get-tuple-element.215, f32[512,512]{1,0:T(8,128)S(1)} %get-tuple-element.220, f32[3,512]{1,0:T(4,128)S(1)} %get-tuple-element.212, ...), kind=kLoop, calls=%fused_computation.9.clone.1 | loop fusion | flops 6288384 | bytes 2134016 | tf_op jit(solution)/shard_map/while/body/eval_jaxpr/while/body/eval_jaxpr/reduce_sum | solution.py:29
  64.4 1.0 %fusion.13 = (f32[512,512]{1,0:T(8,128)S(1)}, f32[512,512]{1,0:T(8,128)S(1)}) fusion(f32[3,512]{1,0:T(4,128)S(1)} %get-tuple-element.212, f32[3,512]{1,0:T(4,128)S(1)} %get-tuple-element.213, f32[3,512]{1,0:T(4,128)S(1)} %get-tuple-element.214, f32[3,512]{1,0:T(4,128)S(1)} %get-tuple-element.215), kind=kLoop, calls=%fused_computation.10.clone.1 | loop fusion | flops 4194304 | bytes 2121728 | tf_op jit(solution)/shard_map/while/body/eval_jaxpr/while/body/eval_jaxpr/reduce_sum | solution.py:28
  65.4 0.3 multiply_multiply_fusion.5
  65.7 1.1 %fusion.14 = (f32[3,512]{1,0:T(4,128)S(1)}, f32[3,512]{1,0:T(4,128)S(1)}) fusion(f32[512,512]{1,0:T(8,128)S(1)} %get-tuple-element.219, f32[3,512]{1,0:T(4,128)S(1)} %get-tuple-element.214, f32[3,512]{1,0:T(4,128)S(1)} %get-tuple-element.215, f32[512,512]{1,0:T(8,128)S(1)} %get-tuple-element.220, f32[3,512]{1,0:T(4,128)S(1)} %get-tuple-element.212, ...), kind=kLoop, calls=%fused_computation.9.clone.1 | loop fusion | flops 6288384 | bytes 2134016 | tf_op jit(solution)/shard_map/while/body/eval_jaxpr/while/body/eval_jaxpr/reduce_sum | solution.py:29
  66.9 14.0 %all_gather.3 = f32[4,7,1536]{2,1,0:T(8,128)S(1)} all-gather(f32[1,7,1536]{2,1,0:T(8,128)S(1)} %bitcast.36), channel_id=1, replica_groups=mesh['grp'=2,'ja'=4,'ia'=4] {'ja'}, dimensions={0}, use_global_device_ids=true | all-gather | bytes 215040 | tf_op jit(solution)/shard_map/all_gather | solution.py:89
  80.9 0.0 copy-done
  80.9 0.0 copy-start.1
  80.9 0.1 multiply_reduce_fusion.3
  81.1 0.1 fusion.6
  81.1 0.6 pad_maximum_fusion.1
  81.8 0.0 copy-done.1
  (46 shorter events, 0.4 us)
Async XLA Ops:
  7.2 43.6 %all-reduce.2.cloned.1.call-start = ((), (), s32[]{:S(2)}) async-start(), calls=%async_computation | async-start | bytes 196608 | tf_op jit(solution)/shard_map/psum | solution.py:87
  9.6 3.1 %copy-start.2 = (s32[1536]{0:T(1024)S(1)}, s32[1536]{0:T(1024)}, u32[]{:S(2)}) copy-start(s32[1536]{0:T(1024)} %param.14) | copy-start | bytes 18436
  9.6 3.1 %copy-start.3 = (s32[1536]{0:T(1024)S(1)}, s32[1536]{0:T(1024)}, u32[]{:S(2)}) copy-start(s32[1536]{0:T(1024)} %param.15) | copy-start | bytes 18436
  9.8 3.6 %copy-start.4 = (f32[1024]{0:T(1024)S(1)}, f32[1024]{0:T(1024)}, u32[]{:S(2)}) copy-start(f32[1024]{0:T(1024)} %param.12) | copy-start | bytes 12292
  51.6 29.3 %copy-start = (f32[13,1536]{1,0:T(8,128)S(1)}, f32[13,1536]{1,0:T(8,128)}, u32[]{:S(2)}) copy-start(f32[13,1536]{1,0:T(8,128)} %all-reduce.2.cloned.1.call-done) | copy-start | bytes 239620
  80.9 0.9 copy-start.1
Sparse Core Ops, SparseCore 0:
  13.5 37.1 all-reduce.1
